TPU v7x, 512 devices: a whole 4x8x8 slice. The times are simulated.
512 devices in a mesh: row: 64 (over y_lo, z, x), col: 8 (over y_hi, core).
Axes of the slice: x: 4, y: 8 (y_hi: 4, y_lo: 2; y = y_hi * 2 + y_lo), z: 8, core: 2. Of those that a mesh axis runs over, the one named last changes fastest.
Arguments:
- orbitals: bfloat16 [16384, 2, 256], P(('row', 'col')), may hold values from -6 to 6
- kernel: bfloat16 [16384, 16384], P('row', 'col'), may hold values from -0.0029296875 to 0.0029296875
- basis: bfloat16 [16384, 2048], P('row'), may hold values from -0.046875 to 0.046875
Outputs:
- exchange: float32 [2048, 2, 256], P('row')
All inputs are finite; a program needn't handle non-finite values.
Results may differ from a plain program's by a relative error of at most 0.0041.
Values may be sent and summed in bfloat16 or wider, within the bound.
A program may use at most 64 MiB of HBM per device.

v0:
```python
import jax
import jax.numpy as jnp
from jax import lax
from jax.sharding import PartitionSpec as P


def body(orbitals, kernel, basis):
    row_orbitals = lax.all_gather(orbitals, "col", axis=0, tiled=True)
    point_rows = row_orbitals.shape[0]
    occupied = orbitals.shape[2]
    column_orbitals = lax.all_gather(orbitals, "row", axis=0, tiled=True)
    density = jnp.einsum(
        "psi,qsi->spq", row_orbitals, column_orbitals, preferred_element_type=jnp.float32
    )
    weighted = (density * kernel[None].astype(jnp.float32)).astype(jnp.bfloat16)
    applied = jnp.einsum(
        "spq,qsi->psi", weighted, column_orbitals, preferred_element_type=jnp.float32
    )
    out_rows = basis.shape[1] // lax.axis_size("row")
    summed = lax.psum(applied, "col").astype(jnp.bfloat16)
    flattened = summed.reshape(point_rows, -1)
    result = lax.psum_scatter(
        lax.dot_general(
            basis, flattened, (((0,), (0,)), ((), ())), preferred_element_type=jnp.float32
        ),
        "row",
        scatter_dimension=0,
        tiled=True,
    )
    return result.reshape(out_rows, 2, occupied)


def solution(mesh):
    return jax.shard_map(
        body,
        mesh=mesh,
        in_specs=(P(("row", "col"), None, None), P("row", "col"), P("row", None)),
        out_specs=P("row", None, None),
        check_vma=False,
    )
```

profile of v0, /device:TPU:40, one launch (start us, length us, event | category | flops | bytes accessed | tf_op | source)
XLA Modules:
  0.0 696.5 jit_solution(10531159770175762090)
XLA Ops:
  6.5 0.0 copy-start
  6.5 0.0 copy-start.1
  6.5 0.0 all-gather.2.cloned.1.call-start
  6.5 1.5 copy.9
  8.0 0.0 all-gather.2.cloned.1.call-update
  8.0 0.0 reduce-scatter.4.cloned.1.call-start
  8.1 1.5 convert_element_type.10
  9.6 0.0 copy-done.1
  9.6 14.6 %all_gather.6 = bf16[256,2,256]{2,1,0:T(2,128)(2,1)S(1)} all-gather(bf16[32,2,256]{2,1,0:T(2,128)(2,1)S(1)} %copy-done.1), channel_id=1, replica_groups=mesh['row'=64,'col'=8] {'col'}, dimensions={0}, use_global_device_ids=true | all-gather | bytes 294912 | tf_op jit(solution)/shard_map/all_gather | solution.py:8
  24.2 292.6 %all-gather.2.cloned.1.call-done = bf16[2048,2,256]{2,0,1:T(8,128)(2,1)} async-done(((bf16[32,2,256]{2,0,1:T(8,128)(2,1)}), bf16[2048,2,256]{2,0,1:T(8,128)(2,1)}) %all-gather.2.cloned.1.call-update) | async-done | bytes 2097168 | tf_op jit(solution)/shard_map/all_gather | solution.py:11
  316.8 4.3 fusion.1
  321.1 35.5 %all-reduce.1 = bf16[256,2,256]{2,0,1:T(8,128)(2,1)S(1)} all-reduce(f32[256,2,256]{2,0,1:T(8,128)} %fusion.1), channel_id=1, replica_groups=mesh['row'=64,'col'=8] {'col'}, use_global_device_ids=true, to_apply=%region_0.0 | all-reduce | flops 131072 | bytes 786432 | tf_op jit(solution)/shard_map/psum | solution.py:20
  356.6 0.1 copy.11
  356.7 0.0 copy-done
  356.7 2.7 convolution_bitcast_fusion
  359.4 5.3 copy.13
  364.8 0.0 reduce-scatter.4.cloned.1.call-update
  364.8 323.2 %reduce-scatter.4.cloned.1.call-done = f32[32,512]{1,0:T(8,128)} async-done(((f32[2048,512]{1,0:T(8,128)}), f32[32,512]{1,0:T(8,128)}) %reduce-scatter.4.cloned.1.call-update) | async-done | bytes 65552
  687.9 1.0 copy.14
  688.9 0.7 copy.12
Async XLA Ops:
  6.5 350.2 %copy-start = (bf16[256,2048]{1,0:T(8,128)(2,1)S(1)}, bf16[256,2048]{1,0:T(8,128)(2,1)}, u32[]{:S(2)}) copy-start(bf16[256,2048]{1,0:T(8,128)(2,1)} %param.5) | copy-start | bytes 3145732
  6.5 3.0 copy-start.1
  6.5 310.2 %all-gather.2.cloned.1.call-start = ((), (), s32[]{:S(2)}) async-start(), calls=%async_computation.1 | async-start | bytes 2129920 | tf_op jit(solution)/shard_map/all_gather | solution.py:11
  8.0 679.9 %reduce-scatter.4.cloned.1.call-start = ((), (), s32[]{:S(2)}) async-start(), calls=%async_computation.2 | async-start | bytes 4259840
Sparse Core Ops, SparseCore 0:
  9.4 307.2 all-gather.1
  364.9 322.9 reduce-scatter.3
where the time goes:
time: 697 us; the launch traced here: 696 us
  waiting for transfers between devices  616 us (88%)
  blocking collectives  50.1 us (7%)
  between operations  13.5 us (2%)
  local copies, waits for them, and re-layouts  8.66 us (1%)
  matrix products  6.99 us (1%)
    unnamed x3, waiting for transfers between devices  323 us
    all_gather x1, waiting for transfers between devices, body(): column_orbitals = lax.all_gather(orbitals, 'row', axis=0, tiled=True)  293 us
    psum x1, blocking collectives, body(): summed = lax.psum(applied, 'col').astype(jnp.bfloat16)  35.5 us
    all_gather x1, blocking collectives, body(): row_orbitals = lax.all_gather(orbitals, 'col', axis=0, tiled=True)  14.6 us
  transfers between devices with their start and end apart: 2, of which 2 were waited for; matrix products, arithmetic and copies ran while one was open for 0% of the time, Pallas kernels for 0%

commit v1 on v0

--- a/solution.py
+++ b/solution.py
@@ -8,7 +8,10 @@
     row_orbitals = lax.all_gather(orbitals, "col", axis=0, tiled=True)
     point_rows = row_orbitals.shape[0]
     occupied = orbitals.shape[2]
-    column_orbitals = lax.all_gather(orbitals, "row", axis=0, tiled=True)
+    detail_shapes = lambda values: jnp.concatenate(
+        lax.all_to_all(jnp.stack([values for _ in range(lax.axis_size("row"))]), "row", 0, 0), 0
+    )
+    column_orbitals = detail_shapes(orbitals)
     density = jnp.einsum(
         "psi,qsi->spq", row_orbitals, column_orbitals, preferred_element_type=jnp.float32
     )

time: 697 us -> 456 us (0.65)
  waiting for transfers between devices: 616 us -> 339 us
  blocking collectives: 50.1 us -> 67.4 us
  starting transfers between devices: 0.04 us -> 14.9 us
    all_gather x1 -> x0, waiting for transfers between devices: 293 us -> none  [body(): column_orbitals = lax.all_gather(orbitals, 'row', axis=0, tiled=True)]
    all_gather x1, blocking collectives: 14.6 us -> 32.7 us  [body(): row_orbitals = lax.all_gather(orbitals, 'col', axis=0, tiled=True)]
    all_to_all x0 -> x1, starting transfers between devices: none -> 14.9 us  [body(): lax.all_to_all(jnp.stack([values for _ in range(lax.axis_size('row'))]),...]
    all_to_all x0 -> x1, waiting for transfers between devices: none -> 13.5 us  [body(): lax.all_to_all(jnp.stack([values for _ in range(lax.axis_size('row'))]),...]
    unnamed x3 -> x2, waiting for transfers between devices: 323 us -> 326 us
  transfers between devices with their start and end apart: 2 -> 2, of which waited for: 2 -> 2; matrix products, arithmetic and copies ran while one was open for 0% -> 1% of each run, Pallas kernels for 0% -> 0%
where the time goes in v1:
time: 456 us
  waiting for transfers between devices  339 us (74%)
  blocking collectives  67.4 us (15%)
  starting transfers between devices  14.9 us (3%)
  between operations  13.5 us (3%)
  local copies, waits for them, and re-layouts  11.1 us (2%)
  matrix products  6.82 us (1%)
    unnamed x2, waiting for transfers between devices  326 us
    psum x1, blocking collectives, body(): summed = lax.psum(applied, 'col').astype(jnp.bfloat16)  34.7 us
    all_gather x1, blocking collectives, body(): row_orbitals = lax.all_gather(orbitals, 'col', axis=0, tiled=True)  32.7 us
    all_to_all x1, starting transfers between devices, body(): lax.all_to_all(jnp.stack([values for _ in range(lax.axis_size('row'))]),...  14.9 us
    all_to_all x1, waiting for transfers between devices, body(): lax.all_to_all(jnp.stack([values for _ in range(lax.axis_size('row'))]),...  13.5 us
  transfers between devices with their start and end apart: 2, of which 2 were waited for; matrix products, arithmetic and copies ran while one was open for 1% of the time, Pallas kernels for 0%

profile of v1, /device:TPU:40, one launch (start us, length us, event | category | flops | bytes accessed | tf_op | source)
XLA Modules:
  0.0 455.6 jit_solution(8143492601367600273)
XLA Ops:
  6.5 0.0 copy-start
  6.5 0.9 copy.9
  7.4 1.6 stack.2
  9.0 14.9 %all-to-all-start = ((bf16[64,32,2,256]{3,1,2,0:T(8,128)(2,1)}), bf16[64,32,2,256]{3,1,2,0:T(8,128)(2,1)S(1)}, u32[]{:S(2)}, u32[]{:S(2)}) async-start(bf16[64,32,2,256]{3,1,2,0:T(8,128)(2,1)} %stack.2), calls=%async_computation | async-start | bytes 4194304 | tf_op jit(solution)/shard_map/all_to_all | solution.py:12
  23.9 0.0 copy-start.1
  23.9 0.0 reduce-scatter.4.cloned.1.call-start
  23.9 2.8 convert_element_type.10
  26.7 0.0 copy-done.1
  26.7 32.7 %all_gather.3 = bf16[256,2,256]{2,1,0:T(2,128)(2,1)S(1)} all-gather(bf16[32,2,256]{2,1,0:T(2,128)(2,1)S(1)} %copy-done.1), channel_id=1, replica_groups=mesh['row'=64,'col'=8] {'col'}, dimensions={0}, use_global_device_ids=true | all-gather | bytes 294912 | tf_op jit(solution)/shard_map/all_gather | solution.py:8
  59.4 13.5 %all-to-all-done = bf16[64,32,2,256]{3,1,2,0:T(8,128)(2,1)S(1)} async-done(((bf16[64,32,2,256]{3,1,2,0:T(8,128)(2,1)}), bf16[64,32,2,256]{3,1,2,0:T(8,128)(2,1)S(1)}, u32[]{:S(2)}, u32[]{:S(2)}) %all-to-all-start) | async-done | bytes 2097184 | tf_op jit(solution)/shard_map/all_to_all | solution.py:12
  72.9 1.5 copy.10
  74.4 4.1 fusion.1
  78.6 34.7 %all-reduce.1 = bf16[256,2,256]{2,0,1:T(8,128)(2,1)S(1)} all-reduce(f32[256,2,256]{2,0,1:T(8,128)S(1)} %fusion.1), channel_id=1, replica_groups=mesh['row'=64,'col'=8] {'col'}, use_global_device_ids=true, to_apply=%region_0.0 | all-reduce | flops 131072 | bytes 786432 | tf_op jit(solution)/shard_map/psum | solution.py:23
  113.3 0.1 copy.12
  113.4 0.0 copy-done
  113.4 2.7 convolution_bitcast_fusion
  116.1 5.3 %copy.14 = f32[2048,512]{1,0:T(8,128)} copy(f32[2048,512]{0,1:T(8,128)} %convolution_bitcast_fusion) | data formatting | bytes 8388608
  121.5 0.0 reduce-scatter.4.cloned.1.call-update
  121.5 325.6 %reduce-scatter.4.cloned.1.call-done = f32[32,512]{1,0:T(8,128)} async-done(((f32[2048,512]{1,0:T(8,128)}), f32[32,512]{1,0:T(8,128)}) %reduce-scatter.4.cloned.1.call-update) | async-done | bytes 65552
  447.1 1.0 copy.15
  448.0 0.7 copy.13
Async XLA Ops:
  6.5 106.9 %copy-start = (bf16[256,2048]{1,0:T(8,128)(2,1)S(1)}, bf16[256,2048]{1,0:T(8,128)(2,1)}, u32[]{:S(2)}) copy-start(bf16[256,2048]{1,0:T(8,128)(2,1)} %param.5) | copy-start | bytes 3145732
  9.0 64.0 %all-to-all-start = ((bf16[64,32,2,256]{3,1,2,0:T(8,128)(2,1)}), bf16[64,32,2,256]{3,1,2,0:T(8,128)(2,1)S(1)}, u32[]{:S(2)}, u32[]{:S(2)}) async-start(bf16[64,32,2,256]{3,1,2,0:T(8,128)(2,1)} %stack.2), calls=%async_computation | async-start | bytes 4194304 | tf_op jit(solution)/shard_map/all_to_all | solution.py:12
  23.9 2.9 copy-start.1
  23.9 423.2 %reduce-scatter.4.cloned.1.call-start = ((), (), s32[]{:S(2)}) async-start(), calls=%async_computation.2 | async-start | bytes 4259840
Sparse Core Ops, SparseCore 0:
  121.6 325.3 reduce-scatter.3
